TPU v7x, 128 devices: a whole 4x4x4 slice. The times are simulated.
128 devices in a mesh: row: 8 (over x, core), col: 16 (over z, y).
Axes of the slice: x: 4, y: 4, z: 4, core: 2. Of those that a mesh axis runs over, the one named last changes fastest.
Arguments:
- tiles: bfloat16 [8, 16, 384, 128, 128], P('row', 'col'), may hold values from -0.15625 to 0.15625
- tile_row: int32 [8, 16, 384], P('row', 'col'), may hold values from 0 to 511, as said below
- tile_col: int32 [8, 16, 384], P('row', 'col'), may hold values from 0 to 255
- tile_count: int32 [8, 16], P('row', 'col'), may hold values from 96 to 384, as said below
- vectors: bfloat16 [32, 8, 16, 4096], P(None, 'row', 'col'), may hold values from -6 to 6
Outputs:
- image: bfloat16 [32, 524288], P(None, ('row', 'col'))
- back_image: bfloat16 [32, 8, 16, 4096], P(None, 'row', 'col')
Inputs may be any that keep to these rules, and one draw needn't show every extreme that they name: `tile_count`: some device has exactly 384 live slots. `tile_row`: the slots of each device, live or not, name exactly 12 distinct block rows in each aligned run of 32 block rows.
All inputs are finite; a program needn't handle non-finite values.
Results may differ from a plain program's by a relative error of at most 0.0041.
Values may be sent and summed in bfloat16 or wider, within the bound.
No kernel may reach another device: no remote copies, remote signals or barrier semaphores. Data moves between devices by JAX's collectives and lax.ppermute only.
A program may use at most 128 MiB of HBM per device.

v0:
```python
import jax
import jax.numpy as jnp
from jax import lax
from jax.sharding import PartitionSpec as P


def per_device(tiles, tile_row, tile_col, tile_count, vectors):
    vec_cols = vectors.shape[0]
    tile_size = tiles.shape[-1]
    slot_count = tiles.shape[2]
    local_tiles = tiles[0, 0]
    rows_local = tile_row[0, 0]
    cols_local = tile_col[0, 0]
    live_count = tile_count[0, 0]
    live_mask = (jnp.arange(slot_count, dtype=jnp.int32) < live_count).astype(jnp.float32)
    row_devices = lax.axis_size("row")
    col_devices = lax.axis_size("col")
    gathered = lax.all_gather(vectors, "row", axis=1, tiled=True)
    blk_cols = gathered.shape[1] * gathered.shape[3] // tile_size
    blk_rows = blk_cols * col_devices // row_devices
    col_vectors = gathered.reshape(vec_cols, blk_cols, tile_size)

    def slot_group():
        return (local_tiles, rows_local, cols_local, live_mask)

    def forward_terms(totals, start_slot, group_size):
        tile_block, row_index, col_index, slot_mask = slot_group()
        picked = jnp.take(col_vectors, col_index, axis=1)
        product = jnp.einsum("ksj,sij->ksi", picked, tile_block, preferred_element_type=jnp.float32)
        return totals.at[:, row_index].add(product * slot_mask[None, :, None])

    def sweep(term_fn, totals_zero):
        return term_fn(totals_zero, 0, slot_count)

    forward_sum = sweep(forward_terms, jnp.zeros((vec_cols, blk_rows, tile_size), jnp.float32))
    partial_rows = forward_sum.reshape(vec_cols, blk_rows * tile_size)
    share_sum = lax.psum_scatter(partial_rows, "col", scatter_dimension=1, tiled=True)
    image = share_sum.astype(jnp.bfloat16)
    row_image = lax.all_gather(image, "col", axis=1, tiled=True)
    row_blocks = row_image.reshape(vec_cols, blk_rows, tile_size)

    def backward_terms(totals, start_slot, group_size):
        tile_block, row_index, col_index, slot_mask = slot_group()
        picked = jnp.take(row_blocks, row_index, axis=1)
        product = jnp.einsum("ksi,sij->ksj", picked, tile_block, preferred_element_type=jnp.float32)
        return totals.at[:, col_index].add(product * slot_mask[None, :, None])

    backward_sum = sweep(backward_terms, jnp.zeros((vec_cols, blk_cols, tile_size), jnp.float32))
    partial_cols = backward_sum.reshape(vec_cols, row_devices, 1, vectors.shape[3])
    back_sum = lax.psum_scatter(partial_cols, "row", scatter_dimension=1, tiled=True)
    return (image, back_sum.astype(jnp.bfloat16))


def solution(mesh):
    return jax.shard_map(
        per_device,
        mesh=mesh,
        in_specs=(
            P("row", "col", None, None, None),
            P("row", "col", None),
            P("row", "col", None),
            P("row", "col"),
            P(None, "row", "col", None),
        ),
        out_specs=(P(None, ("row", "col")), P(None, "row", "col", None)),
        check_vma=False,
    )
```

profile of v0, /device:TPU:0, one launch (start us, length us, event | category | flops | bytes accessed | tf_op | source)
XLA Modules:
  0.0 400.8 jit_solution(5015955300966419793)
XLA Ops:
  7.2 0.0 all-gather.3.cloned.1.call-start
  7.2 0.7 all-gather.3.cloned.1.call-update
  7.9 0.0 reduce-scatter.3.cloned.1.call-start
  8.6 0.7 reduce.1
  9.3 0.7 fusion.22
  10.0 0.7 fusion.21
  10.7 26.6 %all-gather.3.cloned.1.call-done = bf16[32,8,1,4096]{3,0,2,1:T(8,128)(2,1)} async-done(((bf16[32,1,1,4096]{3,0,2,1:T(8,128)(2,1)}), bf16[32,8,1,4096]{3,0,2,1:T(8,128)(2,1)}) %all-gather.3.cloned.1.call-update) | async-done | bytes 2097168 | tf_op jit(solution)/shard_map/all_gather | solution.py:18
  37.3 2.7 copy.18
  40.1 2.4 reshape.89
  42.5 2.9 copy.19
  45.4 3.2 gather_fusion
  48.6 14.9 %broadcast_multiply_fusion.1 = f32[384,32,128]{2,1,0:T(8,128)} fusion(f32[384]{0:T(512)S(1)} %get-tuple-element.6, bf16[1,1,384,128,128]{4,3,2,1,0:T(8,128)(2,1)} %param.5, bf16[384,32,128]{2,1,0:T(8,128)(2,1)} %gather_fusion, pred[384]{0:T(512)(128)(4,1)S(1)} %get-tuple-element.7), kind=kOutput, calls=%fused_computation.15 | convolution fusion | flops 405798912 | bytes 22022016 | tf_op jit(solution)/shard_map/ksj,sij->ksi/dot_general | solution.py:29
  63.5 4.3 %broadcast_in_dim.28 = f32[32,512,128]{2,0,1:T(8,128)} broadcast(f32[]{:T(128)} %constant.18.clone.1), dimensions={} | broadcast | bytes 8388612 | tf_op jit(solution)/shard_map/broadcast_in_dim | solution.py:35
  67.8 51.2 %scatter_fusion = f32[32,512,128]{2,0,1:T(8,128)} fusion(f32[32,512,128]{2,0,1:T(8,128)} %broadcast_in_dim.28, s32[384]{0:T(512)S(1)} %fusion.21, f32[384,32,128]{2,1,0:T(8,128)} %broadcast_multiply_fusion.1), kind=kCustom, calls=%fused_computation.2 | custom fusion | flops 1572864 | bytes 18875904 | tf_op jit(solution)/shard_map/scatter-add | solution.py:30
  119.1 7.1 %copy_bitcast_fusion = f32[32,65536]{1,0:T(8,128)} fusion(f32[32,512,128]{2,0,1:T(8,128)} %scatter_fusion), kind=kLoop, calls=%fused_computation.8 | loop fusion | bytes 16777216 | tf_op jit(solution)/shard_map/reshape | solution.py:36
  126.2 0.0 reduce-scatter.3.cloned.1.call-update
  126.2 0.0 all-gather.5.cloned.1.call-start
  126.3 85.6 %reduce-scatter.3.cloned.1.call-done = f32[32,4096]{1,0:T(8,128)} async-done(((f32[32,65536]{1,0:T(8,128)}), f32[32,4096]{1,0:T(8,128)}) %reduce-scatter.3.cloned.1.call-update) | async-done | bytes 524304 | tf_op jit(solution)/shard_map/reduce_scatter | solution.py:37
  211.8 1.8 convert_element_type.14
  213.6 0.0 all-gather.5.cloned.1.call-update
  213.6 0.2 reduce-scatter.5.cloned.1.call-start
  213.9 51.6 %all-gather.5.cloned.1.call-done = bf16[32,65536]{1,0:T(8,128)(2,1)} async-done(((bf16[32,4096]{1,0:T(8,128)(2,1)}), bf16[32,65536]{1,0:T(8,128)(2,1)}) %all-gather.5.cloned.1.call-update) | async-done | bytes 4194320 | tf_op jit(solution)/shard_map/all_gather | solution.py:39
  265.6 4.9 %copy_bitcast_fusion.1 = bf16[32,512,128]{2,0,1:T(8,128)(2,1)} fusion(bf16[32,65536]{1,0:T(8,128)(2,1)} %all-gather.5.cloned.1.call-done), kind=kLoop, calls=%fused_computation.9 | loop fusion | bytes 8388608 | tf_op jit(solution)/shard_map/reshape | solution.py:40
  270.4 3.4 gather_fusion.1
  273.9 9.0 %broadcast_multiply_fusion = f32[384,32,128]{2,1,0:T(8,128)} fusion(f32[384]{0:T(512)S(1)} %get-tuple-element.6, bf16[1,1,384,128,128]{4,3,2,1,0:T(8,128)(2,1)} %param.5, bf16[384,32,128]{2,1,0:T(8,128)(2,1)S(1)} %gather_fusion.1, pred[384]{0:T(512)(128)(4,1)S(1)} %compare_and_fusion), kind=kOutput, calls=%fused_computation.14 | convolution fusion | flops 405798912 | bytes 22022016 | tf_op jit(solution)/shard_map/ksi,sij->ksj/dot_general | solution.py:45
  282.9 2.6 broadcast_in_dim.31
  285.5 51.3 %scatter_fusion.1 = f32[32,256,128]{2,0,1:T(8,128)} fusion(f32[32,256,128]{2,0,1:T(8,128)} %broadcast_in_dim.31, s32[384]{0:T(512)S(1)} %fusion.22, f32[384,32,128]{2,1,0:T(8,128)} %broadcast_multiply_fusion), kind=kCustom, calls=%fused_computation.3 | custom fusion | flops 1572864 | bytes 18875904 | tf_op jit(solution)/shard_map/scatter-add | solution.py:46
  336.8 6.5 %copy.22 = f32[32,256,128]{2,1,0:T(8,128)} copy(f32[32,256,128]{2,0,1:T(8,128)} %scatter_fusion.1) | data formatting | bytes 8388608 | tf_op jit(solution)/shard_map/scatter-add | solution.py:46
  343.3 5.0 %reshape.92 = f32[32,8,1,4096]{3,1,0,2:T(8,128)} reshape(f32[32,256,128]{2,1,0:T(8,128)} %copy.22) | data formatting | bytes 8388608 | tf_op jit(solution)/shard_map/reshape | solution.py:49
  348.3 6.5 %copy.23 = f32[32,8,1,4096]{3,0,2,1:T(8,128)} copy(f32[32,8,1,4096]{3,1,0,2:T(8,128)} %reshape.92) | data formatting | bytes 8388608 | tf_op jit(solution)/shard_map/reshape | solution.py:49
  354.9 37.6 %reduce-scatter.5.cloned.1.call-done = f32[32,1,1,4096]{3,0,2,1:T(8,128)} async-done(((f32[32,8,1,4096]{3,0,2,1:T(8,128)}), f32[32,1,1,4096]{3,0,2,1:T(8,128)}) %reduce-scatter.5.cloned.1.call-update) | async-done | bytes 524304 | tf_op jit(solution)/shard_map/reduce_scatter | solution.py:50
  392.5 1.8 convert_element_type.15
  (8 shorter events, 0.1 us)
Async XLA Ops:
  7.2 30.2 %all-gather.3.cloned.1.call-start = ((), (), s32[]{:S(2)}) async-start(), calls=%async_computation.2 | async-start | bytes 2359296 | tf_op jit(solution)/shard_map/all_gather | solution.py:18
  7.9 203.9 %reduce-scatter.3.cloned.1.call-start = ((), (), s32[]{:S(2)}) async-start(), calls=%async_computation.3 | async-start | bytes 8912896 | tf_op jit(solution)/shard_map/reduce_scatter | solution.py:37
  126.2 87.7 %copy-start = (s32[1,1,384]{2,1,0:T(1,128)S(1)}, s32[1,1,384]{2,1,0:T(1,128)}, u32[]{:S(2)}) copy-start(s32[1,1,384]{2,1,0:T(1,128)} %param.6) | copy-start | bytes 4612
  126.2 139.3 %all-gather.5.cloned.1.call-start = ((), (), s32[]{:S(2)}) async-start(), calls=%async_computation.4 | async-start | bytes 4456448 | tf_op jit(solution)/shard_map/all_gather | solution.py:39
  213.6 178.8 %reduce-scatter.5.cloned.1.call-start = ((), (), s32[]{:S(2)}) async-start(), calls=%async_computation.5 | async-start | bytes 4718592 | tf_op jit(solution)/shard_map/reduce_scatter | solution.py:50
Sparse Core Ops, SparseCore 0:
  9.7 27.5 all-gather.2
  126.3 85.4 reduce-scatter.2
  214.6 50.9 all-gather.4
  355.0 37.4 reduce-scatter.4
where the time goes:
time: 402 us; the launch traced here: 401 us
  waiting for transfers between devices  202 us (50%)
  other arithmetic  108 us (27%)
  local copies, waits for them, and re-layouts  51.6 us (13%)
  matrix products  24 us (6%)
  between operations  14.4 us (4%)
    reduce_scatter x1, waiting for transfers between devices, per_device(): lax.psum_scatter(partial_rows, 'col', scatter_dimension=1, tiled=True)  85.6 us
    all_gather x1, waiting for transfers between devices, per_device(): row_image = lax.all_gather(image, 'col', axis=1, tiled=True)  51.6 us
    scatter-add x1, other arithmetic, backward_terms(): return totals.at[:, col_index].add(product * slot_mask[None, :, None])  51.3 us
    scatter-add x1, other arithmetic, forward_terms(): return totals.at[:, row_index].add(product * slot_mask[None, :, None])  51.2 us
    reduce_scatter x1, waiting for transfers between devices, per_device(): lax.psum_scatter(partial_cols, 'row', scatter_dimension=1, tiled=True)  37.6 us
    all_gather x1, waiting for transfers between devices, per_device(): gathered = lax.all_gather(vectors, 'row', axis=1, tiled=True)  26.6 us
    dot_general x1, matrix products, forward_terms(): jnp.einsum('ksj,sij->ksi', picked, tile_block, preferred_element_type=jnp...  14.9 us
    reshape x2, local copies, waits for them, and re-layouts, per_device(): backward_sum.reshape(vec_cols, row_devices, 1, vectors.shape[3])  11.5 us
  transfers between devices with their start and end apart: 4, of which 4 were waited for; matrix products, arithmetic and copies ran while one was open for 1% of the time, Pallas kernels for 0%

commit v1 on v0

--- a/solution.py
+++ b/solution.py
@@ -15,7 +15,31 @@
     live_mask = (jnp.arange(slot_count, dtype=jnp.int32) < live_count).astype(jnp.float32)
     row_devices = lax.axis_size("row")
     col_devices = lax.axis_size("col")
-    gathered = lax.all_gather(vectors, "row", axis=1, tiled=True)
+    local_out = lax.axis_size("row")
+    d_next = lax.axis_index("row")
+    placed, before, part_now = (local_out, d_next, vectors.shape[1])
+    lanes = []
+    for no, it in enumerate(vectors.shape):
+        lanes.append(it * placed if no == 1 else it)
+    latest = jnp.zeros(lanes, vectors.dtype)
+    gathered = lax.dynamic_update_slice_in_dim(latest, vectors, before * part_now, axis=1)
+    r1 = mixed_arr = vectors
+    for hop_no in range(1, placed // 2 + 1):
+        kept_rows = []
+        for no in range(placed):
+            kept_rows.append((no, (no + 1) % placed))
+        r1 = lax.ppermute(r1, axis_name="row", perm=kept_rows)
+        gathered = lax.dynamic_update_slice_in_dim(
+            gathered, r1, (before - hop_no) % placed * part_now, axis=1
+        )
+        if 2 * hop_no < placed:
+            all_blocks = []
+            for no in range(placed):
+                all_blocks.append((no, (no - 1) % placed))
+            mixed_arr = lax.ppermute(mixed_arr, axis_name="row", perm=all_blocks)
+            gathered = lax.dynamic_update_slice_in_dim(
+                gathered, mixed_arr, (before + hop_no) % placed * part_now, axis=1
+            )
     blk_cols = gathered.shape[1] * gathered.shape[3] // tile_size
     blk_rows = blk_cols * col_devices // row_devices
     col_vectors = gathered.reshape(vec_cols, blk_cols, tile_size)

time: 402 us -> 444 us (1.10)
  local copies, waits for them, and re-layouts: 51.6 us -> 98.5 us
  waiting for transfers between devices: 202 us -> 188 us
  starting transfers between devices: 0.34 us -> 8.98 us
    dynamic_update_slice x0 -> x8, local copies, waits for them, and re-layouts: none -> 40.3 us  [the longest x4 20.1 us: per_device(): lax.dynamic_update_slice_in_dim(gathered, r1, (before - hop_no) % placed...]
    all_gather x1 -> x0, waiting for transfers between devices: 26.6 us -> none  [per_device(): gathered = lax.all_gather(vectors, 'row', axis=1, tiled=True)]
    ppermute x0 -> x7, waiting for transfers between devices: none -> 11 us  [the longest x4 10.9 us: per_device(): r1 = lax.ppermute(r1, axis_name='row', perm=kept_rows)]
    ppermute x0 -> x7, starting transfers between devices: none -> 8.86 us  [the longest x3 8.83 us: per_device(): mixed_arr = lax.ppermute(mixed_arr, axis_name='row', perm=all_blocks)]
    ppermute x0 -> x7, local copies, waits for them, and re-layouts: none -> 7.64 us  [the longest x4 5.05 us: per_device(): r1 = lax.ppermute(r1, axis_name='row', perm=kept_rows)]
  transfers between devices with their start and end apart: 4 -> 10, of which waited for: 4 -> 6; matrix products, arithmetic and copies ran while one was open for 1% -> 10% of each run, Pallas kernels for 0% -> 0%
where the time goes in v1:
time: 444 us; the launch traced here: 443 us
  waiting for transfers between devices  188 us (42%)
  other arithmetic  108 us (24%)
  local copies, waits for them, and re-layouts  98.5 us (22%)
  matrix products  24 us (5%)
  between operations  14.8 us (3%)
  starting transfers between devices  8.98 us (2%)
    reduce_scatter x1, waiting for transfers between devices, per_device(): lax.psum_scatter(partial_rows, 'col', scatter_dimension=1, tiled=True)  87.7 us
    all_gather x1, waiting for transfers between devices, per_device(): row_image = lax.all_gather(image, 'col', axis=1, tiled=True)  51.8 us
    scatter-add x1, other arithmetic, backward_terms(): return totals.at[:, col_index].add(product * slot_mask[None, :, None])  51.3 us
    scatter-add x1, other arithmetic, forward_terms(): return totals.at[:, row_index].add(product * slot_mask[None, :, None])  51.2 us
    reduce_scatter x1, waiting for transfers between devices, per_device(): lax.psum_scatter(partial_cols, 'row', scatter_dimension=1, tiled=True)  37.6 us
    dynamic_update_slice x4, local copies, waits for them, and re-layouts, per_device(): lax.dynamic_update_slice_in_dim(gathered, r1, (before - hop_no) % placed...  20.1 us
    dynamic_update_slice x3, local copies, waits for them, and re-layouts, per_device(): lax.dynamic_update_slice_in_dim(gathered, mixed_arr, (before + hop_no) %...  15.1 us
    dot_general x1, matrix products, forward_terms(): jnp.einsum('ksj,sij->ksi', picked, tile_block, preferred_element_type=jnp...  14.9 us
  transfers between devices with their start and end apart: 10, of which 6 were waited for; matrix products, arithmetic and copies ran while one was open for 10% of the time, Pallas kernels for 0%

profile of v1, /device:TPU:0, one launch (start us, length us, event | category | flops | bytes accessed | tf_op | source)
XLA Modules:
  0.0 442.6 jit_solution(10380057657508186000)
XLA Ops:
  7.2 2.9 collective-permute-start.1
  10.2 4.3 collective-permute-done
  14.4 3.0 collective-permute-start.3
  17.4 4.0 collective-permute-done.2
  22.9 2.9 collective-permute-start.5
  25.8 2.6 collective-permute-done.4
  31.7 5.0 %dynamic_update_slice.24 = bf16[32,8,1,4096]{3,1,0,2:T(8,128)(2,1)S(1)} dynamic-update-slice(bf16[32,8,1,4096]{3,1,0,2:T(8,128)(2,1)S(1)} %broadcast_in_dim.33, bf16[32,1,1,4096]{3,1,0,2:T(2,128)(2,1)S(1)} %copy.32, s32[]{:T(128)} %constant.78.clone.1, s32[]{:T(128)S(6)} %select_n.98, s32[]{:T(128)} %constant.78.clone.1, s32[]{:T(128)} %constant.78.clone.1) | dynamic-update-slice | bytes 524292 | tf_op jit(solution)/shard_map/dynamic_update_slice | solution.py:25
  38.3 5.0 %dynamic_update_slice.25 = bf16[32,8,1,4096]{3,1,0,2:T(8,128)(2,1)S(1)} dynamic-update-slice(bf16[32,8,1,4096]{3,1,0,2:T(8,128)(2,1)S(1)} %dynamic_update_slice.24, bf16[32,1,1,4096]{3,1,0,2:T(2,128)(2,1)S(1)} %copy.33, s32[]{:T(128)} %constant.78.clone.1, s32[]{:T(128)S(6)} %select_n.100, s32[]{:T(128)} %constant.78.clone.1, s32[]{:T(128)} %constant.78.clone.1) | dynamic-update-slice | bytes 524292 | tf_op jit(solution)/shard_map/dynamic_update_slice | solution.py:32
  43.9 5.0 %dynamic_update_slice.26 = bf16[32,8,1,4096]{3,1,0,2:T(8,128)(2,1)S(1)} dynamic-update-slice(bf16[32,8,1,4096]{3,1,0,2:T(8,128)(2,1)S(1)} %dynamic_update_slice.25, bf16[32,1,1,4096]{3,1,0,2:T(2,128)(2,1)S(1)} %copy.34, s32[]{:T(128)} %constant.78.clone.1, s32[]{:T(128)S(6)} %select_n.102, s32[]{:T(128)} %constant.78.clone.1, s32[]{:T(128)} %constant.78.clone.1) | dynamic-update-slice | bytes 524292 | tf_op jit(solution)/shard_map/dynamic_update_slice | solution.py:40
  50.5 5.0 %dynamic_update_slice.27 = bf16[32,8,1,4096]{3,1,0,2:T(8,128)(2,1)S(1)} dynamic-update-slice(bf16[32,8,1,4096]{3,1,0,2:T(8,128)(2,1)S(1)} %dynamic_update_slice.26, bf16[32,1,1,4096]{3,1,0,2:T(2,128)(2,1)S(1)} %copy.35, s32[]{:T(128)} %constant.78.clone.1, s32[]{:T(128)S(6)} %select_n.104, s32[]{:T(128)} %constant.78.clone.1, s32[]{:T(128)} %constant.78.clone.1) | dynamic-update-slice | bytes 524292 | tf_op jit(solution)/shard_map/dynamic_update_slice | solution.py:32
  56.1 5.0 %dynamic_update_slice.28 = bf16[32,8,1,4096]{3,1,0,2:T(8,128)(2,1)S(1)} dynamic-update-slice(bf16[32,8,1,4096]{3,1,0,2:T(8,128)(2,1)S(1)} %dynamic_update_slice.27, bf16[32,1,1,4096]{3,1,0,2:T(2,128)(2,1)S(1)} %copy.36, s32[]{:T(128)} %constant.78.clone.1, s32[]{:T(128)S(6)} %select_n.106, s32[]{:T(128)} %constant.78.clone.1, s32[]{:T(128)} %constant.78.clone.1) | dynamic-update-slice | bytes 524292 | tf_op jit(solution)/shard_map/dynamic_update_slice | solution.py:40
  61.7 5.0 %dynamic_update_slice.29 = bf16[32,8,1,4096]{3,1,0,2:T(8,128)(2,1)S(1)} dynamic-update-slice(bf16[32,8,1,4096]{3,1,0,2:T(8,128)(2,1)S(1)} %dynamic_update_slice.28, bf16[32,1,1,4096]{3,1,0,2:T(2,128)(2,1)S(1)} %copy.37, s32[]{:T(128)} %constant.78.clone.1, s32[]{:T(128)S(6)} %select_n.108, s32[]{:T(128)} %constant.78.clone.1, s32[]{:T(128)} %constant.78.clone.1) | dynamic-update-slice | bytes 524292 | tf_op jit(solution)/shard_map/dynamic_update_slice | solution.py:32
  68.2 5.0 %dynamic_update_slice.30 = bf16[32,8,1,4096]{3,1,0,2:T(8,128)(2,1)S(1)} dynamic-update-slice(bf16[32,8,1,4096]{3,1,0,2:T(8,128)(2,1)S(1)} %dynamic_update_slice.29, bf16[32,1,1,4096]{3,1,0,2:T(2,128)(2,1)S(1)} %copy.38, s32[]{:T(128)} %constant.78.clone.1, s32[]{:T(128)S(6)} %select_n.110, s32[]{:T(128)} %constant.78.clone.1, s32[]{:T(128)} %constant.78.clone.1) | dynamic-update-slice | bytes 524292 | tf_op jit(solution)/shard_map/dynamic_update_slice | solution.py:40
  74.8 5.0 %dynamic_update_slice.31 = bf16[32,8,1,4096]{3,1,0,2:T(8,128)(2,1)S(1)} dynamic-update-slice(bf16[32,8,1,4096]{3,1,0,2:T(8,128)(2,1)S(1)} %dynamic_update_slice.30, bf16[32,1,1,4096]{3,1,0,2:T(2,128)(2,1)S(1)} %copy.39, s32[]{:T(128)} %constant.78.clone.1, s32[]{:T(128)S(6)} %select_n.112, s32[]{:T(128)} %constant.78.clone.1, s32[]{:T(128)} %constant.78.clone.1) | dynamic-update-slice | bytes 524292 | tf_op jit(solution)/shard_map/dynamic_update_slice | solution.py:32
  79.8 2.4 reshape.89
  82.2 2.9 copy.40
  85.1 3.2 gather_fusion
  88.3 14.9 %broadcast_multiply_fusion.1 = f32[384,32,128]{2,1,0:T(8,128)} fusion(f32[384]{0:T(512)S(1)} %get-tuple-element.6, bf16[1,1,384,128,128]{4,3,2,1,0:T(8,128)(2,1)} %param.5, bf16[384,32,128]{2,1,0:T(8,128)(2,1)} %gather_fusion, pred[384]{0:T(512)(128)(4,1)S(1)} %get-tuple-element.7), kind=kOutput, calls=%fused_computation.15 | convolution fusion | flops 405798912 | bytes 22022016 | tf_op jit(solution)/shard_map/ksj,sij->ksi/dot_general | solution.py:53
  103.3 4.3 broadcast_in_dim.31
  107.6 51.2 %scatter_fusion = f32[32,512,128]{2,0,1:T(8,128)} fusion(f32[32,512,128]{2,0,1:T(8,128)} %broadcast_in_dim.31, s32[384]{0:T(512)S(1)} %fusion.21, f32[384,32,128]{2,1,0:T(8,128)} %broadcast_multiply_fusion.1), kind=kCustom, calls=%fused_computation.2 | custom fusion | flops 1572864 | bytes 18875904 | tf_op jit(solution)/shard_map/scatter-add | solution.py:54
  158.8 7.1 %copy_bitcast_fusion = f32[32,65536]{1,0:T(8,128)} fusion(f32[32,512,128]{2,0,1:T(8,128)} %scatter_fusion), kind=kLoop, calls=%fused_computation.8 | loop fusion | bytes 16777216 | tf_op jit(solution)/shard_map/reshape | solution.py:60
  166.0 87.7 %reduce-scatter.3.cloned.1.call-done = f32[32,4096]{1,0:T(8,128)} async-done(((f32[32,65536]{1,0:T(8,128)}), f32[32,4096]{1,0:T(8,128)}) %reduce-scatter.3.cloned.1.call-update) | async-done | bytes 524304 | tf_op jit(solution)/shard_map/reduce_scatter | solution.py:61
  255.6 51.8 %all-gather.2.cloned.1.call-done = bf16[32,65536]{1,0:T(8,128)(2,1)} async-done(((bf16[32,4096]{1,0:T(8,128)(2,1)}), bf16[32,65536]{1,0:T(8,128)(2,1)}) %all-gather.2.cloned.1.call-update) | async-done | bytes 4194320 | tf_op jit(solution)/shard_map/all_gather | solution.py:63
  307.4 4.9 %copy_bitcast_fusion.1 = bf16[32,512,128]{2,0,1:T(8,128)(2,1)} fusion(bf16[32,65536]{1,0:T(8,128)(2,1)} %all-gather.2.cloned.1.call-done), kind=kLoop, calls=%fused_computation.9 | loop fusion | bytes 8388608 | tf_op jit(solution)/shard_map/reshape | solution.py:64
  312.3 3.4 gather_fusion.1
  315.7 9.0 %broadcast_multiply_fusion = f32[384,32,128]{2,1,0:T(8,128)} fusion(f32[384]{0:T(512)S(1)} %get-tuple-element.6, bf16[1,1,384,128,128]{4,3,2,1,0:T(8,128)(2,1)} %param.5, bf16[384,32,128]{2,1,0:T(8,128)(2,1)S(1)} %gather_fusion.1, pred[384]{0:T(512)(128)(4,1)S(1)} %compare_and_fusion), kind=kOutput, calls=%fused_computation.14 | convolution fusion | flops 405798912 | bytes 22022016 | tf_op jit(solution)/shard_map/ksi,sij->ksj/dot_general | solution.py:69
  324.7 2.6 broadcast_in_dim.35
  327.3 51.3 %scatter_fusion.1 = f32[32,256,128]{2,0,1:T(8,128)} fusion(f32[32,256,128]{2,0,1:T(8,128)} %broadcast_in_dim.35, s32[384]{0:T(512)S(1)} %fusion.22, f32[384,32,128]{2,1,0:T(8,128)} %broadcast_multiply_fusion), kind=kCustom, calls=%fused_computation.3 | custom fusion | flops 1572864 | bytes 18875904 | tf_op jit(solution)/shard_map/scatter-add | solution.py:70
  378.6 6.5 %copy.43 = f32[32,256,128]{2,1,0:T(8,128)} copy(f32[32,256,128]{2,0,1:T(8,128)} %scatter_fusion.1) | data formatting | bytes 8388608 | tf_op jit(solution)/shard_map/scatter-add | solution.py:70
  385.2 5.0 %reshape.92 = f32[32,8,1,4096]{3,1,0,2:T(8,128)} reshape(f32[32,256,128]{2,1,0:T(8,128)} %copy.43) | data formatting | bytes 8388608 | tf_op jit(solution)/shard_map/reshape | solution.py:73
  390.1 6.5 %copy.44 = f32[32,8,1,4096]{3,0,2,1:T(8,128)} copy(f32[32,8,1,4096]{3,1,0,2:T(8,128)} %reshape.92) | data formatting | bytes 8388608 | tf_op jit(solution)/shard_map/reshape | solution.py:73
  396.7 37.6 %reduce-scatter.5.cloned.1.call-done = f32[32,1,1,4096]{3,0,2,1:T(8,128)} async-done(((f32[32,8,1,4096]{3,0,2,1:T(8,128)}), f32[32,1,1,4096]{3,0,2,1:T(8,128)}) %reduce-scatter.5.cloned.1.call-update) | async-done | bytes 524304 | tf_op jit(solution)/shard_map/reduce_scatter | solution.py:74
  (39 shorter events, 15.3 us)
Async XLA Ops:
  7.2 246.5 %reduce-scatter.3.cloned.1.call-start = ((), (), s32[]{:S(2)}) async-start(), calls=%async_computation.2 | async-start | bytes 8912896 | tf_op jit(solution)/shard_map/reduce_scatter | solution.py:61
  7.2 7.2 %collective-permute-start = (bf16[32,1,1,4096]{3,0,2,1:T(8,128)(2,1)}, bf16[32,1,1,4096]{3,0,2,1:T(8,128)(2,1)S(1)}, u32[]{:S(2)}, u32[]{:S(2)}) collective-permute-start(bf16[32,1,1,4096]{3,0,2,1:T(8,128)(2,1)} %param.9), channel_id=1, source_target_pairs={{0,16},{16,32},{32,48},{48,64},{64,80},{80,96},{96,112},{112,0},{1... | collective-permute-start | bytes 786440 | tf_op jit(solution)/shard_map/ppermute | solution.py:31
  7.2 7.2 %collective-permute-start.1 = (bf16[32,1,1,4096]{3,0,2,1:T(8,128)(2,1)}, bf16[32,1,1,4096]{3,0,2,1:T(8,128)(2,1)S(1)}, u32[]{:S(2)}, u32[]{:S(2)}) collective-permute-start(bf16[32,1,1,4096]{3,0,2,1:T(8,128)(2,1)} %param.9), channel_id=1, source_target_pairs={{0,112},{16,0},{32,16},{48,32},{64,48},{80,64},{96,80},{112,96},{1... | collective-permute-start | bytes 786440 | tf_op jit(solution)/shard_map/ppermute | solution.py:39
  14.4 7.0 %copy-start.1 = (bf16[32,1,1,4096]{3,0,2,1:T(8,128)(2,1)}, bf16[32,1,1,4096]{3,0,2,1:T(8,128)(2,1)S(1)}, u32[]{:S(2)}) copy-start(bf16[32,1,1,4096]{3,0,2,1:T(8,128)(2,1)S(1)} %collective-permute-done) | copy-start | bytes 786436
  14.4 7.0 %collective-permute-start.2 = (bf16[32,1,1,4096]{3,0,2,1:T(8,128)(2,1)S(1)}, bf16[32,1,1,4096]{3,0,2,1:T(8,128)(2,1)S(1)}, u32[]{:S(2)}, u32[]{:S(2)}) collective-permute-start(bf16[32,1,1,4096]{3,0,2,1:T(8,128)(2,1)S(1)} %collective-permute-done), channel_id=1, source_target_pairs={{0,16},{16,32},{32,48},{48,64},{64,80},{80,96},{96,112},{112,0},{1... | collective-permute-start | bytes 786440 | tf_op jit(solution)/shard_map/ppermute | solution.py:31
  14.4 8.4 %collective-permute-start.3 = (bf16[32,1,1,4096]{3,0,2,1:T(8,128)(2,1)S(1)}, bf16[32,1,1,4096]{3,0,2,1:T(8,128)(2,1)S(1)}, u32[]{:S(2)}, u32[]{:S(2)}) collective-permute-start(bf16[32,1,1,4096]{3,0,2,1:T(8,128)(2,1)S(1)} %collective-permute-done.1), channel_id=1, source_target_pairs={{0,112},{16,0},{32,16},{48,32},{64,48},{80,64},{96,80},{112,96},{1... | collective-permute-start | bytes 786440 | tf_op jit(solution)/shard_map/ppermute | solution.py:39
  21.5 7.0 %copy-start = (bf16[32,1,1,4096]{3,0,2,1:T(8,128)(2,1)}, bf16[32,1,1,4096]{3,0,2,1:T(8,128)(2,1)S(1)}, u32[]{:S(2)}) copy-start(bf16[32,1,1,4096]{3,0,2,1:T(8,128)(2,1)S(1)} %collective-permute-done.2) | copy-start | bytes 786436
  21.5 7.0 %collective-permute-start.4 = (bf16[32,1,1,4096]{3,0,2,1:T(8,128)(2,1)S(1)}, bf16[32,1,1,4096]{3,0,2,1:T(8,128)(2,1)S(1)}, u32[]{:S(2)}, u32[]{:S(2)}) collective-permute-start(bf16[32,1,1,4096]{3,0,2,1:T(8,128)(2,1)S(1)} %collective-permute-done.2), channel_id=1, source_target_pairs={{0,16},{16,32},{32,48},{48,64},{64,80},{80,96},{96,112},{112,0},{1... | collective-permute-start | bytes 786440 | tf_op jit(solution)/shard_map/ppermute | solution.py:31
  22.9 43.8 %collective-permute-start.5 = (bf16[32,1,1,4096]{3,0,2,1:T(8,128)(2,1)S(1)}, bf16[32,1,1,4096]{3,0,2,1:T(8,128)(2,1)}, u32[]{:S(2)}, u32[]{:S(2)}) collective-permute-start(bf16[32,1,1,4096]{3,0,2,1:T(8,128)(2,1)S(1)} %collective-permute-done.3), channel_id=1, source_target_pairs={{0,112},{16,0},{32,16},{48,32},{64,48},{80,64},{96,80},{112,96},{1... | collective-permute-start | bytes 786440 | tf_op jit(solution)/shard_map/ppermute | solution.py:39
  28.5 44.8 %collective-permute-start.6 = (bf16[32,1,1,4096]{3,0,2,1:T(8,128)(2,1)S(1)}, bf16[32,1,1,4096]{3,0,2,1:T(8,128)(2,1)}, u32[]{:S(2)}, u32[]{:S(2)}) collective-permute-start(bf16[32,1,1,4096]{3,0,2,1:T(8,128)(2,1)S(1)} %collective-permute-done.4), channel_id=1, source_target_pairs={{0,16},{16,32},{32,48},{48,64},{64,80},{80,96},{96,112},{112,0},{1... | collective-permute-start | bytes 786440 | tf_op jit(solution)/shard_map/ppermute | solution.py:31
  165.9 89.6 %copy-start.2 = (s32[1,1,384]{2,1,0:T(1,128)S(1)}, s32[1,1,384]{2,1,0:T(1,128)}, u32[]{:S(2)}) copy-start(s32[1,1,384]{2,1,0:T(1,128)} %param.6) | copy-start | bytes 4612
  166.0 141.4 %all-gather.2.cloned.1.call-start = ((), (), s32[]{:S(2)}) async-start(), calls=%async_computation.3 | async-start | bytes 4456448 | tf_op jit(solution)/shard_map/all_gather | solution.py:63
  255.5 178.8 %reduce-scatter.5.cloned.1.call-start = ((), (), s32[]{:S(2)}) async-start(), calls=%async_computation.4 | async-start | bytes 4718592 | tf_op jit(solution)/shard_map/reduce_scatter | solution.py:74
Sparse Core Ops, SparseCore 0:
  166.1 87.5 reduce-scatter.2
  256.4 50.9 all-gather.1
  396.8 37.4 reduce-scatter.4
